TPU v7x, 32 devices: a whole 2x2x4 slice. The times are simulated.
32 devices in a mesh: group: 4 (over z), vf: 8 (over y, x, core).
Axes of the slice: x: 2, y: 2, z: 4, core: 2. Of those that a mesh axis runs over, the one named last changes fastest.
Arguments:
- query_rows: bfloat16 [32, 512, 1536], P(('group', 'vf')), may hold values from -28 to 28
- key_value: bfloat16 [32, 2, 512, 1536], P(('group', 'vf')), may hold values from -8 to 8
- out_weight: bfloat16 [1536, 1536], replicated, may hold values from -0.15625 to 0.15625
- partners: int32 [8, 6], replicated, may hold values from -1 to 7, as said below
Outputs:
- mixed: bfloat16 [32, 512, 1536], P(('group', 'vf'))
Inputs may be any that keep to these rules, and one draw needn't show every extreme that they name: Row v lists the distinct partners of view v, each of the form (v + d) mod 8 for an offset d in -3 to 3 other than 0, followed by -1 in the slots left over; the relation is symmetric; every view has 1 to 6 partners and some view has 6.
All inputs are finite; a program needn't handle non-finite values.
Results may differ from a plain program's by a relative error of at most 0.0052.
Values may be sent and summed in bfloat16 or wider, within the bound.
A program may use at most 128 MiB of HBM per device.

v0:
```python
import math

import jax
import jax.numpy as jnp
from jax import lax
from jax.experimental import pallas as pl
from jax.experimental.pallas import tpu as pltpu
from jax.sharding import PartitionSpec as P

HEADS = 12
HEAD_DIM = 128
FRAMES = 4
OFFSETS = (0, -3, -2, -1, 1, 2, 3)
SCALE = math.log2(math.e) / math.sqrt(HEAD_DIM)
FAR = 1e30
MESH = pl.DeviceIdType.MESH


def attend_rows(query, keys, values, gap, scores):
    tokens = keys(0).shape[0]
    running = None
    for b in range(len(OFFSETS)):
        block = lax.dot_general(
            query, keys(b), (((1,), (1,)), ((), ())), preferred_element_type=jnp.float32
        )
        scores[:, b * tokens : (b + 1) * tokens] = block
        lanes = block[:, :HEAD_DIM]
        for c in range(HEAD_DIM, tokens, HEAD_DIM):
            lanes = jnp.maximum(lanes, block[:, c : c + HEAD_DIM])
        running = lanes if b == 0 else jnp.maximum(running, lanes - gap(b))
    row_max = jnp.max(running, axis=1, keepdims=True) * SCALE
    total = None
    ones = jnp.ones((tokens, HEAD_DIM), jnp.bfloat16)
    for b in range(len(OFFSETS)):
        shift = row_max if b == 0 else row_max + gap(b)
        exponent = jnp.exp2(scores[:, b * tokens : (b + 1) * tokens] * SCALE - shift)
        part = jnp.dot(
            exponent.astype(jnp.bfloat16),
            jnp.concatenate([values(b), ones], axis=1),
            preferred_element_type=jnp.float32,
        )
        total = part if total is None else total + part
    return total[:, :HEAD_DIM] / total[:, HEAD_DIM:]


def local(query_rows, key_value, out_weight, partners):
    groups = lax.axis_size("group")
    members = lax.axis_size("vf")
    local_views = members // FRAMES
    tokens, features = query_rows.shape[1:]
    heads = features // HEAD_DIM // groups
    rows = tokens // 2
    view_count = groups * local_views
    shifts = [0]
    slots = []
    for offset in OFFSETS:
        if offset % local_views not in shifts:
            shifts.append(offset % local_views)
        slots.append(shifts.index(offset % local_views))
    relays = shifts[1:]
    order = sorted(range(1, groups), key=lambda r: abs(2 * r - groups))

    def kernel(
        partners_ref, query_hbm, pair_hbm, weight_hbm, out_ref,
        queries, pairs, outs, gathered, weights, scores, total, squares,
        query_send, query_recv, pair_send, pair_recv, relay_send, relay_recv,
        out_send, out_recv, local_sem, weight_sem,
    ):
        mine = lax.axis_index("group")
        member = lax.axis_index("vf")
        view = member // FRAMES

        def partner(group, b):
            shifted = group * local_views + view + OFFSETS[b] + view_count
            return lax.rem(shifted, view_count)

        def gap(group, b):
            row = group * local_views + view
            gap = jnp.float32(FAR)
            for slot in range(partners_ref.shape[1]):
                gap = jnp.where(partners_ref[row, slot] == partner(group, b), 0.0, gap)
            return gap

        def columns(group, h):
            return pl.ds(pl.multiple_of((group * heads + h) * HEAD_DIM, HEAD_DIM), HEAD_DIM)

        def ahead(r):
            return lax.rem(mine + r, groups)

        def query_copy(h, r):
            return pltpu.make_async_remote_copy(
                src_ref=query_hbm.at[0, :, columns(ahead(r), h)],
                dst_ref=queries.at[h, mine],
                send_sem=query_send.at[h, r - 1],
                recv_sem=query_recv.at[h, r - 1],
                device_id={"group": ahead(r)},
                device_id_type=MESH,
            )

        def pair_copy(h, r):
            return pltpu.make_async_remote_copy(
                src_ref=pair_hbm.at[0, :, :, columns(ahead(r), h)],
                dst_ref=pairs.at[0, h, mine],
                send_sem=pair_send.at[h, r - 1],
                recv_sem=pair_recv.at[h, r - 1],
                device_id={"group": ahead(r)},
                device_id_type=MESH,
            )

        def relay_copy(h, r, i):
            origin = lax.rem(mine + groups - r, groups)
            source = pair_hbm.at[0, :, :, columns(mine, h)] if r == 0 else pairs.at[0, h, origin]
            return pltpu.make_async_remote_copy(
                src_ref=source,
                dst_ref=pairs.at[i + 1, h, origin],
                send_sem=relay_send.at[h, i, r],
                recv_sem=relay_recv.at[h, i, r],
                device_id={"vf": lax.rem(member + members - relays[i] * FRAMES, members)},
                device_id_type=MESH,
            )

        def own_copies(h):
            return (
                pltpu.make_async_copy(
                    query_hbm.at[0, :, columns(mine, h)], queries.at[h, mine], local_sem.at[h, 0]
                ),
                pltpu.make_async_copy(
                    pair_hbm.at[0, :, :, columns(mine, h)], pairs.at[0, h, mine], local_sem.at[h, 1]
                ),
            )

        def out_copy(h, r):
            return pltpu.make_async_remote_copy(
                src_ref=outs.at[h, ahead(r)],
                dst_ref=gathered.at[h, :, pl.ds(pl.multiple_of(mine * HEAD_DIM, HEAD_DIM), HEAD_DIM)],
                send_sem=out_send.at[h, r],
                recv_sem=out_recv.at[h, r],
                device_id={"group": ahead(r)},
                device_id_type=MESH,
            )

        def own_out(h):
            return pltpu.make_async_copy(
                outs.at[h, mine],
                gathered.at[h, :, pl.ds(pl.multiple_of(mine * HEAD_DIM, HEAD_DIM), HEAD_DIM)],
                local_sem.at[h, 2],
            )

        def weight_copy(h, group):
            return pltpu.make_async_copy(
                weight_hbm.at[pl.ds((group * heads + h) * HEAD_DIM, HEAD_DIM)],
                weights.at[h, pl.ds(group * HEAD_DIM, HEAD_DIM)],
                weight_sem.at[h, group],
            )

        barrier = pltpu.get_barrier_semaphore()
        for r in range(1, groups):
            pl.semaphore_signal(barrier, inc=1, device_id={"group": ahead(r)}, device_id_type=MESH)
        for shift in relays:
            neighbour = lax.rem(member + shift * FRAMES, members)
            pl.semaphore_signal(barrier, inc=1, device_id={"vf": neighbour}, device_id_type=MESH)
        pl.semaphore_wait(barrier, groups - 1 + len(relays))

        for h in range(heads):
            for r in order:
                pair_copy(h, r).start()
            for r in order:
                query_copy(h, r).start()
            for copy in own_copies(h):
                copy.start()
            for i in range(len(relays)):
                relay_copy(h, 0, i).start()
        for h in range(heads):
            for group in range(groups):
                weight_copy(h, group).start()

        @pl.loop(0, heads)
        def _(h):
            for r in order:
                pair_copy(h, r).wait_recv()
                for i in range(len(relays)):
                    relay_copy(h, r, i).start()
            for r in order:
                query_copy(h, r).wait_recv()
            for copy in own_copies(h):
                copy.wait()

            @pl.when(h == heads - 1)
            def _():
                for earlier in range(heads - 1):
                    for r in order:
                        out_copy(earlier, r).start()

            for r in [0] + order:
                for i in range(len(relays)):
                    relay_copy(h, r, i).wait_recv()

            @pl.loop(0, groups)
            def _(step):
                r = lax.rem(step + 1, groups)
                target = ahead(r)

                def source(b):
                    return partner(target, b) // local_views

                sources = [source(b) for b in range(len(OFFSETS))]
                gaps = [gap(target, b) for b in range(len(OFFSETS))]
                for part in range(0, tokens, rows):
                    outs[h, target, part : part + rows] = attend_rows(
                        queries[h, target, part : part + rows],
                        lambda b: pairs[slots[b], h, sources[b], 0],
                        lambda b: pairs[slots[b], h, sources[b], 1],
                        lambda b: gaps[b],
                        scores.at[part // rows],
                    ).astype(outs.dtype)

                @pl.when((step < groups - 1) & (h == heads - 1))
                def _():
                    out_copy(h, r).start()

                @pl.when(step == groups - 1)
                def _():
                    own_out(h).start()

        total[...] = jnp.zeros_like(total)
        squares[...] = jnp.zeros_like(squares)

        @pl.loop(0, heads)
        def _(h):
            own_out(h).wait()
            for r in range(1, groups):
                out_copy(h, r).wait_recv()
            for group in range(groups):
                weight_copy(h, group).wait()
            width = groups * HEAD_DIM
            for c in range(0, width, HEAD_DIM):
                block = gathered[h, :, c : c + HEAD_DIM].astype(jnp.float32)
                squares[...] += block * block

            @pl.loop(0, features, step=width)
            def _(c):
                strip = pl.ds(pl.multiple_of(c, width), width)
                total[:, strip] += jnp.dot(
                    gathered[h], weights[h, :, strip], preferred_element_type=jnp.float32
                )

        mean = jnp.sum(squares[...], axis=1, keepdims=True) * (1.0 / features)
        out_ref[0] = (total[...] * lax.rsqrt(mean + 1e-06)).astype(out_ref.dtype)

        @pl.loop(0, heads)
        def _(h):
            for r in range(1, groups):
                query_copy(h, r).wait_send()
                pair_copy(h, r).wait_send()
                out_copy(h, r).wait_send()
            for r in range(groups):
                for i in range(len(relays)):
                    relay_copy(h, r, i).wait_send()

    hbm = pl.BlockSpec(memory_space=pl.ANY)
    dma = pltpu.SemaphoreType.DMA
    bf16 = jnp.bfloat16
    return pl.pallas_call(
        kernel,
        out_shape=jax.ShapeDtypeStruct(query_rows.shape, bf16),
        in_specs=[pl.BlockSpec(memory_space=pltpu.SMEM), hbm, hbm, hbm],
        out_specs=pl.BlockSpec(memory_space=pltpu.VMEM),
        scratch_shapes=[
            pltpu.VMEM((heads, groups, tokens, HEAD_DIM), bf16),
            pltpu.VMEM((len(shifts), heads, groups, 2, tokens, HEAD_DIM), bf16),
            pltpu.VMEM((heads, groups, tokens, HEAD_DIM), bf16),
            pltpu.VMEM((heads, tokens, groups * HEAD_DIM), bf16),
            pltpu.VMEM((heads, groups * HEAD_DIM, features), bf16),
            pltpu.VMEM((2, rows, tokens * len(OFFSETS)), jnp.float32),
            pltpu.VMEM((tokens, features), jnp.float32),
            pltpu.VMEM((tokens, HEAD_DIM), jnp.float32),
            dma((heads, groups - 1)),
            dma((heads, groups - 1)),
            dma((heads, groups - 1)),
            dma((heads, groups - 1)),
            dma((heads, len(relays), groups)),
            dma((heads, len(relays), groups)),
            dma((heads, groups)),
            dma((heads, groups)),
            dma((heads, 3)),
            dma((heads, groups)),
        ],
        compiler_params=pltpu.CompilerParams(
            collective_id=0, has_side_effects=True, vmem_limit_bytes=62 << 20
        ),
    )(partners, query_rows, key_value, out_weight)


def solution(mesh):
    placed = (P(("group", "vf"), None, None), P(("group", "vf"), None, None, None), P(), P())
    return jax.shard_map(
        local, mesh=mesh, in_specs=placed, out_specs=P(("group", "vf"), None, None), check_vma=False
    )
```

profile of v0, /device:TPU:16, one launch (start us, length us, event | category | flops | bytes accessed | tf_op | source)
XLA Modules:
  0.0 149.0 jit_solution(16280801869799247143)
XLA Ops:
  0.0 146.3 %shard_map.46 = bf16[1,512,1536]{2,1,0:T(8,128)(2,1)} custom-call(s32[8,6]{1,0:T(8,128)} %partners_ref.1, bf16[1,512,1536]{2,1,0:T(8,128)(2,1)} %query_hbm.1, bf16[1,2,512,1536]{3,2,1,0:T(8,128)(2,1)} %pair_hbm.1, bf16[1536,1536]{1,0:T(8,128)(2,1)} %weight_hbm.1), custom_call_target="tpu_custom_call" | custom-call | tf_op jit(solution)/shard_map/pallas_call | solution.py:263
  146.3 2.7 %copy.6 = bf16[1,512,1536]{2,1,0:T(8,128)(2,1)} copy(bf16[1,512,1536]{2,1,0:T(8,128)(2,1)} %shard_map.46) | data formatting | bytes 3145728
where the time goes:
time: 149 us
  Pallas kernels  146 us (98%)
  local copies, waits for them, and re-layouts  2.65 us (2%)
    pallas_call x1, Pallas kernels, local(): pl.pallas_call(kernel, out_shape=jax.ShapeDtypeStruct(query_rows.shape, b...  146 us

commit v1 on v0

--- a/solution.py
+++ b/solution.py
@@ -13,6 +13,7 @@
 OFFSETS = (0, -3, -2, -1, 1, 2, 3)
 SCALE = math.log2(math.e) / math.sqrt(HEAD_DIM)
 FAR = 1e30
+SPARE = 6 << 20
 MESH = pl.DeviceIdType.MESH
 
 
@@ -49,7 +50,8 @@
     local_views = members // FRAMES
     tokens, features = query_rows.shape[1:]
     heads = features // HEAD_DIM // groups
-    rows = tokens // 2
+    parts = 2
+    rows = tokens // parts
     view_count = groups * local_views
     shifts = [0]
     slots = []
@@ -61,10 +63,10 @@
     order = sorted(range(1, groups), key=lambda r: abs(2 * r - groups))
 
     def kernel(
-        partners_ref, query_hbm, pair_hbm, weight_hbm, out_ref,
-        queries, pairs, outs, gathered, weights, scores, total, squares,
+        partners_hbm, query_hbm, pair_hbm, weight_hbm, out_ref,
+        partners_ref, queries, pairs, outs, gathered, weights, scores, total, squares,
         query_send, query_recv, pair_send, pair_recv, relay_send, relay_recv,
-        out_send, out_recv, local_sem, weight_sem,
+        out_send, out_recv, local_sem, weight_sem, partners_sem, below, above,
     ):
         mine = lax.axis_index("group")
         member = lax.axis_index("vf")
@@ -129,21 +131,23 @@
                 ),
             )
 
-        def out_copy(h, r):
+        def my_columns():
+            return pl.ds(pl.multiple_of(mine * HEAD_DIM, HEAD_DIM), HEAD_DIM)
+
+        def out_copy(h, r, part):
+            strip = pl.ds(part * rows, rows)
             return pltpu.make_async_remote_copy(
-                src_ref=outs.at[h, ahead(r)],
-                dst_ref=gathered.at[h, :, pl.ds(pl.multiple_of(mine * HEAD_DIM, HEAD_DIM), HEAD_DIM)],
-                send_sem=out_send.at[h, r],
-                recv_sem=out_recv.at[h, r],
+                src_ref=outs.at[h, ahead(r), strip],
+                dst_ref=gathered.at[h, strip, my_columns()],
+                send_sem=out_send.at[h, r, part],
+                recv_sem=out_recv.at[h, r, part],
                 device_id={"group": ahead(r)},
                 device_id_type=MESH,
             )
 
         def own_out(h):
             return pltpu.make_async_copy(
-                outs.at[h, mine],
-                gathered.at[h, :, pl.ds(pl.multiple_of(mine * HEAD_DIM, HEAD_DIM), HEAD_DIM)],
-                local_sem.at[h, 2],
+                outs.at[h, mine], gathered.at[h, :, my_columns()], local_sem.at[h, 2]
             )
 
         def weight_copy(h, group):
@@ -153,26 +157,73 @@
                 weight_sem.at[h, group],
             )
 
+        def line_neighbours(act):
+            @pl.when(mine > 0)
+            def _():
+                act(mine - 1)
+
+            @pl.when(mine < groups - 1)
+            def _():
+                act(mine + 1)
+
         barrier = pltpu.get_barrier_semaphore()
-        for r in range(1, groups):
-            pl.semaphore_signal(barrier, inc=1, device_id={"group": ahead(r)}, device_id_type=MESH)
+        line_neighbours(
+            lambda group: pl.semaphore_signal(barrier, inc=1, device_id={"group": group}, device_id_type=MESH)
+        )
         for shift in relays:
             neighbour = lax.rem(member + shift * FRAMES, members)
             pl.semaphore_signal(barrier, inc=1, device_id={"vf": neighbour}, device_id_type=MESH)
-        pl.semaphore_wait(barrier, groups - 1 + len(relays))
+        load_partners = pltpu.make_async_copy(partners_hbm, partners_ref, partners_sem)
+        load_partners.start()
+        for h in range(heads):
+            for copy in own_copies(h):
+                copy.start()
+        beside = (mine > 0).astype(jnp.int32) + (mine < groups - 1).astype(jnp.int32)
+        pl.semaphore_wait(barrier, beside + len(relays))
+
+        def near(r):
+            if r == 1:
+                return (mine < groups - 1) | (mine > 0) if groups == 2 else mine < groups - 1
+            return mine > 0 if r == groups - 1 else None
+
+        for r in order:
+            if near(r) is not None:
+                pl.when(near(r))(pair_copy(0, r).start)
+        for i in range(len(relays)):
+            relay_copy(0, 0, i).start()
+
+        for k in range(2, groups):
+            @pl.when((mine - (k - 1) >= 0) & (mine + 1 < groups))
+            def _():
+                pl.semaphore_signal(below.at[k], inc=1, device_id={"group": mine + 1}, device_id_type=MESH)
+
+            @pl.when((mine + (k - 1) < groups) & (mine > 0))
+            def _():
+                pl.semaphore_signal(above.at[k], inc=1, device_id={"group": mine - 1}, device_id_type=MESH)
+
+            @pl.when(mine - k >= 0)
+            def _():
+                pl.semaphore_wait(below.at[k], 1)
+
+            @pl.when(mine + k < groups)
+            def _():
+                pl.semaphore_wait(above.at[k], 1)
 
         for h in range(heads):
             for r in order:
-                pair_copy(h, r).start()
+                if h > 0 or near(r) is None:
+                    pair_copy(h, r).start()
+                else:
+                    pl.when(jnp.logical_not(near(r)))(pair_copy(h, r).start)
             for r in order:
                 query_copy(h, r).start()
-            for copy in own_copies(h):
-                copy.start()
-            for i in range(len(relays)):
-                relay_copy(h, 0, i).start()
+            if h > 0:
+                for i in range(len(relays)):
+                    relay_copy(h, 0, i).start()
         for h in range(heads):
             for group in range(groups):
                 weight_copy(h, group).start()
+        load_partners.wait()
 
         @pl.loop(0, heads)
         def _(h):
@@ -189,7 +240,8 @@
             def _():
                 for earlier in range(heads - 1):
                     for r in order:
-                        out_copy(earlier, r).start()
+                        for part in range(parts):
+                            out_copy(earlier, r, part).start()
 
             for r in [0] + order:
                 for i in range(len(relays)):
@@ -205,18 +257,20 @@
 
                 sources = [source(b) for b in range(len(OFFSETS))]
                 gaps = [gap(target, b) for b in range(len(OFFSETS))]
-                for part in range(0, tokens, rows):
-                    outs[h, target, part : part + rows] = attend_rows(
-                        queries[h, target, part : part + rows],
+                for part in range(parts):
+                    strip = pl.ds(part * rows, rows)
+                    outs[h, target, strip] = attend_rows(
+                        queries[h, target, strip],
                         lambda b: pairs[slots[b], h, sources[b], 0],
                         lambda b: pairs[slots[b], h, sources[b], 1],
                         lambda b: gaps[b],
-                        scores.at[part // rows],
+                        scores.at[part],
                     ).astype(outs.dtype)
 
                 @pl.when((step < groups - 1) & (h == heads - 1))
                 def _():
-                    out_copy(h, r).start()
+                    for part in range(parts):
+                        out_copy(h, r, part).start()
 
                 @pl.when(step == groups - 1)
                 def _():
@@ -224,18 +278,24 @@
 
         total[...] = jnp.zeros_like(total)
         squares[...] = jnp.zeros_like(squares)
-
-        @pl.loop(0, heads)
-        def _(h):
+        width = groups * HEAD_DIM
+
+        def square(h, strip):
+            for c in range(0, width, HEAD_DIM):
+                block = gathered[h, strip, c : c + HEAD_DIM].astype(jnp.float32)
+                squares[strip] += block * block
+
+        for h in range(heads):
             own_out(h).wait()
-            for r in range(1, groups):
-                out_copy(h, r).wait_recv()
             for group in range(groups):
                 weight_copy(h, group).wait()
-            width = groups * HEAD_DIM
-            for c in range(0, width, HEAD_DIM):
-                block = gathered[h, :, c : c + HEAD_DIM].astype(jnp.float32)
-                squares[...] += block * block
+
+        @pl.loop(0, heads - 1)
+        def _(h):
+            for r in range(1, groups):
+                for part in range(parts):
+                    out_copy(h, r, part).wait_recv()
+            square(h, pl.ds(0, tokens))
 
             @pl.loop(0, features, step=width)
             def _(c):
@@ -244,15 +304,29 @@
                     gathered[h], weights[h, :, strip], preferred_element_type=jnp.float32
                 )
 
-        mean = jnp.sum(squares[...], axis=1, keepdims=True) * (1.0 / features)
-        out_ref[0] = (total[...] * lax.rsqrt(mean + 1e-06)).astype(out_ref.dtype)
+        last = heads - 1
+        for part in range(parts):
+            for r in range(1, groups):
+                out_copy(last, r, part).wait_recv()
+            strip = pl.ds(part * rows, rows)
+            square(last, strip)
+            mean = jnp.sum(squares[strip], axis=1, keepdims=True) * (1.0 / features)
+            scale = lax.rsqrt(mean + 1e-06)
+            for c in range(0, features, width):
+                block = jnp.dot(
+                    gathered[last, strip], weights[last, :, c : c + width], preferred_element_type=jnp.float32
+                )
+                out_ref[0, strip, c : c + width] = ((total[strip, c : c + width] + block) * scale).astype(
+                    out_ref.dtype
+                )
 
         @pl.loop(0, heads)
         def _(h):
             for r in range(1, groups):
                 query_copy(h, r).wait_send()
                 pair_copy(h, r).wait_send()
-                out_copy(h, r).wait_send()
+                for part in range(parts):
+                    out_copy(h, r, part).wait_send()
             for r in range(groups):
                 for i in range(len(relays)):
                     relay_copy(h, r, i).wait_send()
@@ -260,35 +334,48 @@
     hbm = pl.BlockSpec(memory_space=pl.ANY)
     dma = pltpu.SemaphoreType.DMA
     bf16 = jnp.bfloat16
+    buffers = [
+        ((heads, groups, tokens, HEAD_DIM), bf16),
+        ((len(shifts), heads, groups, 2, tokens, HEAD_DIM), bf16),
+        ((heads, groups, tokens, HEAD_DIM), bf16),
+        ((heads, tokens, groups * HEAD_DIM), bf16),
+        ((heads, groups * HEAD_DIM, features), bf16),
+        ((parts, rows, tokens * len(OFFSETS)), jnp.float32),
+        ((tokens, features), jnp.float32),
+        ((tokens, HEAD_DIM), jnp.float32),
+    ]
+    held = sum(math.prod(shape) * jnp.dtype(dtype).itemsize for shape, dtype in buffers)
     return pl.pallas_call(
         kernel,
         out_shape=jax.ShapeDtypeStruct(query_rows.shape, bf16),
-        in_specs=[pl.BlockSpec(memory_space=pltpu.SMEM), hbm, hbm, hbm],
+        in_specs=[hbm, hbm, hbm, hbm],
         out_specs=pl.BlockSpec(memory_space=pltpu.VMEM),
         scratch_shapes=[
-            pltpu.VMEM((heads, groups, tokens, HEAD_DIM), bf16),
-            pltpu.VMEM((len(shifts), heads, groups, 2, tokens, HEAD_DIM), bf16),
-            pltpu.VMEM((heads, groups, tokens, HEAD_DIM), bf16),
-            pltpu.VMEM((heads, tokens, groups * HEAD_DIM), bf16),
-            pltpu.VMEM((heads, groups * HEAD_DIM, features), bf16),
-            pltpu.VMEM((2, rows, tokens * len(OFFSETS)), jnp.float32),
-            pltpu.VMEM((tokens, features), jnp.float32),
-            pltpu.VMEM((tokens, HEAD_DIM), jnp.float32),
+            pltpu.SMEM(partners.shape, partners.dtype),
+            *(pltpu.VMEM(shape, dtype) for shape, dtype in buffers),
             dma((heads, groups - 1)),
             dma((heads, groups - 1)),
             dma((heads, groups - 1)),
             dma((heads, groups - 1)),
             dma((heads, len(relays), groups)),
             dma((heads, len(relays), groups)),
-            dma((heads, groups)),
-            dma((heads, groups)),
+            dma((heads, groups, parts)),
+            dma((heads, groups, parts)),
             dma((heads, 3)),
             dma((heads, groups)),
+            dma(()),
+            pltpu.SemaphoreType.REGULAR((groups,)),
+            pltpu.SemaphoreType.REGULAR((groups,)),
         ],
         compiler_params=pltpu.CompilerParams(
-            collective_id=0, has_side_effects=True, vmem_limit_bytes=62 << 20
+            collective_id=0, has_side_effects=True, vmem_limit_bytes=held + SPARE
         ),
-    )(partners, query_rows, key_value, out_weight)
+    )(
+        *(
+            pltpu.with_memory_space_constraint(array, pltpu.HBM)
+            for array in (partners, query_rows, key_value, out_weight)
+        )
+    )
 
 
 def solution(mesh):

time: 149 us -> 144 us (0.966)
  Pallas kernels: 146 us -> 143 us
  local copies, waits for them, and re-layouts: 2.65 us -> 1.15 us
    pallas_call x1, Pallas kernels: 146 us -> 143 us  [local(): pl.pallas_call(kernel, out_shape=jax.ShapeDtypeStruct(query_rows.shape, b...]
    unnamed x1, local copies, waits for them, and re-layouts: 2.65 us -> 1.15 us
where the time goes in v1:
time: 144 us
  Pallas kernels  143 us (99%)
    pallas_call x1, Pallas kernels, local(): pl.pallas_call(kernel, out_shape=jax.ShapeDtypeStruct(query_rows.shape, b...  143 us

profile of v1, /device:TPU:16, one launch (start us, length us, event | category | flops | bytes accessed | tf_op | source)
XLA Modules:
  0.0 144.0 jit_solution(624550466221968007)
XLA Ops:
  0.0 142.8 %shard_map.46 = bf16[1,512,1536]{2,1,0:T(8,128)(2,1)S(1)} custom-call(s32[8,6]{1,0:T(8,128)} %partners_hbm.1, bf16[1,512,1536]{2,1,0:T(8,128)(2,1)} %query_hbm.1, bf16[1,2,512,1536]{3,2,1,0:T(8,128)(2,1)} %pair_hbm.1, bf16[1536,1536]{1,0:T(8,128)(2,1)} %weight_hbm.1), custom_call_target="tpu_custom_call" | custom-call | tf_op jit(solution)/shard_map/pallas_call | solution.py:348
  142.8 1.1 copy.6

commit v2 on v1

--- a/solution.py
+++ b/solution.py
@@ -60,7 +60,26 @@
             shifts.append(offset % local_views)
         slots.append(shifts.index(offset % local_views))
     relays = shifts[1:]
-    order = sorted(range(1, groups), key=lambda r: abs(2 * r - groups))
+    turns = range(groups - 1)
+    inner_groups = ((groups - 1) // 2, groups // 2)
+
+    def crosses(group, other):
+        return (2 * group >= groups) != (2 * other >= groups)
+
+    send_turns = [
+        sorted(
+            range(1, groups),
+            key=lambda r: (not crosses(group, (group + r) % groups), -abs((group + r) % groups - group)),
+        )
+        for group in range(groups)
+    ]
+    wait_turns = [
+        sorted(
+            range(1, groups),
+            key=lambda r: crosses(group, (group - r) % groups) and (group - r) % groups in inner_groups,
+        )
+        for group in range(groups)
+    ]
 
     def kernel(
         partners_hbm, query_hbm, pair_hbm, weight_hbm, out_ref,
@@ -89,6 +108,13 @@
         def ahead(r):
             return lax.rem(mine + r, groups)
 
+        def turn(table, i):
+            return sum((mine == group).astype(jnp.int32) * table[group][i] for group in range(groups))
+
+        to = [turn(send_turns, i) for i in turns]
+        heard = [turn(wait_turns, i) for i in turns]
+        inner = (mine == inner_groups[0]) | (mine == inner_groups[1])
+
         def query_copy(h, r):
             return pltpu.make_async_remote_copy(
                 src_ref=query_hbm.at[0, :, columns(ahead(r), h)],
@@ -111,7 +137,7 @@
 
         def relay_copy(h, r, i):
             origin = lax.rem(mine + groups - r, groups)
-            source = pair_hbm.at[0, :, :, columns(mine, h)] if r == 0 else pairs.at[0, h, origin]
+            source = pair_hbm.at[0, :, :, columns(mine, h)] if isinstance(r, int) and r == 0 else pairs.at[0, h, origin]
             return pltpu.make_async_remote_copy(
                 src_ref=source,
                 dst_ref=pairs.at[i + 1, h, origin],
@@ -181,14 +207,14 @@
         beside = (mine > 0).astype(jnp.int32) + (mine < groups - 1).astype(jnp.int32)
         pl.semaphore_wait(barrier, beside + len(relays))
 
+        beside_above = mine < groups - 1
+        beside_below = mine > 0
+
         def near(r):
-            if r == 1:
-                return (mine < groups - 1) | (mine > 0) if groups == 2 else mine < groups - 1
-            return mine > 0 if r == groups - 1 else None
-
-        for r in order:
-            if near(r) is not None:
-                pl.when(near(r))(pair_copy(0, r).start)
+            return ((r == 1) & beside_above) | ((r == groups - 1) & beside_below)
+
+        for r in to:
+            pl.when(near(r))(pair_copy(0, r).start)
         for i in range(len(relays)):
             relay_copy(0, 0, i).start()
 
@@ -209,17 +235,30 @@
             def _():
                 pl.semaphore_wait(above.at[k], 1)
 
-        for h in range(heads):
-            for r in order:
-                if h > 0 or near(r) is None:
-                    pair_copy(h, r).start()
-                else:
-                    pl.when(jnp.logical_not(near(r)))(pair_copy(h, r).start)
-            for r in order:
+        def send_head(h):
+            for r in to:
+                pair_copy(h, r).start()
+            for r in to:
                 query_copy(h, r).start()
-            if h > 0:
-                for i in range(len(relays)):
-                    relay_copy(h, 0, i).start()
+
+        def send_outs(h):
+            for r in to:
+                for part in range(parts):
+                    out_copy(h, r, part).start()
+
+        for r in to:
+            pl.when(jnp.logical_not(near(r)))(pair_copy(0, r).start)
+        for r in to:
+            query_copy(0, r).start()
+
+        @pl.when(inner)
+        def _():
+            for h in range(1, heads):
+                send_head(h)
+
+        for h in range(1, heads):
+            for i in range(len(relays)):
+                relay_copy(h, 0, i).start()
         for h in range(heads):
             for group in range(groups):
                 weight_copy(h, group).start()
@@ -227,29 +266,31 @@
 
         @pl.loop(0, heads)
         def _(h):
-            for r in order:
+            for r in heard:
                 pair_copy(h, r).wait_recv()
                 for i in range(len(relays)):
                     relay_copy(h, r, i).start()
-            for r in order:
+            for r in heard:
                 query_copy(h, r).wait_recv()
             for copy in own_copies(h):
                 copy.wait()
 
-            @pl.when(h == heads - 1)
+            @pl.when(jnp.logical_not(inner) & (h < heads - 1))
+            def _():
+                send_head(h + 1)
+
+            @pl.when(jnp.logical_not(inner) & (h == heads - 1))
             def _():
                 for earlier in range(heads - 1):
-                    for r in order:
-                        for part in range(parts):
-                            out_copy(earlier, r, part).start()
-
-            for r in [0] + order:
+                    send_outs(earlier)
+
+            for r in [0] + heard:
                 for i in range(len(relays)):
                     relay_copy(h, r, i).wait_recv()
 
             @pl.loop(0, groups)
             def _(step):
-                r = lax.rem(step + 1, groups)
+                r = sum((step == i).astype(jnp.int32) * to[i] for i in turns)
                 target = ahead(r)
 
                 def source(b):
@@ -275,6 +316,10 @@
                 @pl.when(step == groups - 1)
                 def _():
                     own_out(h).start()
+
+            @pl.when(inner & (h < heads - 1))
+            def _():
+                send_outs(h)
 
         total[...] = jnp.zeros_like(total)
         squares[...] = jnp.zeros_like(squares)

time: 144 us -> 143 us (level); the launches traced: 144 us -> 141 us
  Pallas kernels: 143 us -> 139 us
    pallas_call x1, Pallas kernels: 143 us -> 139 us  [local(): pl.pallas_call(kernel, out_shape=jax.ShapeDtypeStruct(query_rows.shape, b...]
where the time goes in v2:
time: 143 us; the launch traced here: 141 us
  Pallas kernels  139 us (97%)
    pallas_call x1, Pallas kernels, local(): pl.pallas_call(kernel, out_shape=jax.ShapeDtypeStruct(query_rows.shape, b...  139 us

profile of v2, /device:TPU:16, one launch (start us, length us, event | category | flops | bytes accessed | tf_op | source)
XLA Modules:
  0.0 140.6 jit_solution(11786953563399231237)
XLA Ops:
  0.0 139.4 %shard_map.46 = bf16[1,512,1536]{2,1,0:T(8,128)(2,1)S(1)} custom-call(s32[8,6]{1,0:T(8,128)} %partners_hbm.1, bf16[1,512,1536]{2,1,0:T(8,128)(2,1)} %query_hbm.1, bf16[1,2,512,1536]{3,2,1,0:T(8,128)(2,1)} %pair_hbm.1, bf16[1536,1536]{1,0:T(8,128)(2,1)} %weight_hbm.1), custom_call_target="tpu_custom_call" | custom-call | tf_op jit(solution)/shard_map/pallas_call | solution.py:393
  139.4 1.1 copy.6

commit v3 on v2

--- a/solution.py
+++ b/solution.py
@@ -66,6 +66,12 @@
     def crosses(group, other):
         return (2 * group >= groups) != (2 * other >= groups)
 
+    def towards_middle(group):
+        return group + 1 if 2 * group + 1 < groups else group - 1 if 2 * group + 1 > groups else -1
+
+    parents = [towards_middle(group) for group in range(groups)]
+    children = [[other for other in range(groups) if parents[other] == group] for group in range(groups)]
+
     send_turns = [
         sorted(
             range(1, groups),
@@ -113,6 +119,7 @@
 
         to = [turn(send_turns, i) for i in turns]
         heard = [turn(wait_turns, i) for i in turns]
+        parent = sum((mine == group).astype(jnp.int32) * parents[group] for group in range(groups))
         inner = (mine == inner_groups[0]) | (mine == inner_groups[1])
 
         def query_copy(h, r):
@@ -183,19 +190,16 @@
                 weight_sem.at[h, group],
             )
 
-        def line_neighbours(act):
-            @pl.when(mine > 0)
-            def _():
-                act(mine - 1)
-
-            @pl.when(mine < groups - 1)
-            def _():
-                act(mine + 1)
+        def tell(semaphore, group):
+            pl.semaphore_signal(semaphore, inc=1, device_id={"group": group}, device_id_type=MESH)
+
+        def among(members_of):
+            return sum(((mine == group).astype(jnp.int32) for group in members_of), jnp.int32(0)) > 0
 
         barrier = pltpu.get_barrier_semaphore()
-        line_neighbours(
-            lambda group: pl.semaphore_signal(barrier, inc=1, device_id={"group": group}, device_id_type=MESH)
-        )
+        for step in (-1, 1):
+            telling = [g for g in range(groups) if g + step in children[g]]
+            pl.when(among(telling))(lambda step=step: tell(barrier, mine + step))
         for shift in relays:
             neighbour = lax.rem(member + shift * FRAMES, members)
             pl.semaphore_signal(barrier, inc=1, device_id={"vf": neighbour}, device_id_type=MESH)
@@ -204,28 +208,30 @@
         for h in range(heads):
             for copy in own_copies(h):
                 copy.start()
-        beside = (mine > 0).astype(jnp.int32) + (mine < groups - 1).astype(jnp.int32)
-        pl.semaphore_wait(barrier, beside + len(relays))
-
-        beside_above = mine < groups - 1
-        beside_below = mine > 0
+        pl.semaphore_wait(barrier, (parent >= 0).astype(jnp.int32) + len(relays))
 
         def near(r):
-            return ((r == 1) & beside_above) | ((r == groups - 1) & beside_below)
+            return ahead(r) == parent
 
         for r in to:
             pl.when(near(r))(pair_copy(0, r).start)
         for i in range(len(relays)):
             relay_copy(0, 0, i).start()
 
+        for step, semaphore in ((1, below), (-1, above)):
+            reporting = [g for g in range(groups) if parents[g] == g + step and parents[g + step] != g]
+            hearing = [g + step for g in reporting]
+            pl.when(among(reporting))(lambda step=step, semaphore=semaphore: tell(semaphore.at[1], mine + step))
+            pl.when(among(hearing))(lambda semaphore=semaphore: pl.semaphore_wait(semaphore.at[1], 1))
+
         for k in range(2, groups):
             @pl.when((mine - (k - 1) >= 0) & (mine + 1 < groups))
             def _():
-                pl.semaphore_signal(below.at[k], inc=1, device_id={"group": mine + 1}, device_id_type=MESH)
+                tell(below.at[k], mine + 1)
 
             @pl.when((mine + (k - 1) < groups) & (mine > 0))
             def _():
-                pl.semaphore_signal(above.at[k], inc=1, device_id={"group": mine - 1}, device_id_type=MESH)
+                tell(above.at[k], mine - 1)
 
             @pl.when(mine - k >= 0)
             def _():

time: 143 us -> 143 us (level)
  no operation moved by 1% of the time
where the time goes in v3:
time: 143 us; the launch traced here: 141 us
  Pallas kernels  139 us (97%)
    pallas_call x1, Pallas kernels, local(): pl.pallas_call(kernel, out_shape=jax.ShapeDtypeStruct(query_rows.shape, b...  139 us

profile of v3, /device:TPU:16, one launch (start us, length us, event | category | flops | bytes accessed | tf_op | source)
XLA Modules:
  0.0 140.6 jit_solution(941481894971504479)
XLA Ops:
  0.0 139.4 %shard_map.46 = bf16[1,512,1536]{2,1,0:T(8,128)(2,1)S(1)} custom-call(s32[8,6]{1,0:T(8,128)} %partners_hbm.1, bf16[1,512,1536]{2,1,0:T(8,128)(2,1)} %query_hbm.1, bf16[1,2,512,1536]{3,2,1,0:T(8,128)(2,1)} %pair_hbm.1, bf16[1536,1536]{1,0:T(8,128)(2,1)} %weight_hbm.1), custom_call_target="tpu_custom_call" | custom-call | tf_op jit(solution)/shard_map/pallas_call | solution.py:399
  139.4 1.1 copy.6
